TPU v7x, 32 devices: a whole 2x2x4 slice. The times are simulated.
32 devices in a mesh: dp: 4 (over z), expert: 8 (over y, x, core).
Axes of the slice: x: 2, y: 2, z: 4, core: 2. Of those that a mesh axis runs over, the one named last changes fastest.
Arguments:
- out_grad: bfloat16 [8192, 4096], P(('dp', 'expert')), may hold values from -6 to 6
- destination: int32 [8192, 1], P(('dp', 'expert')), may hold values from 0 to 7; in each aligned block of 256 rows (0 to 255, 256 to 511, ...) at most 64 rows name the same one
- hidden: bfloat16 [16384, 1024], P(('dp', 'expert')), may hold values from -6 to 6
- weight: bfloat16 [8, 1024, 4096], P('expert', None, 'dp'), may hold values from -0.09375 to 0.09375
- left_prev: float32 [8, 2048, 1024], P('expert', 'dp'), may hold values from -3 to 3
- right_prev: float32 [8, 4096, 2048], P('expert', 'dp'), may hold values from -3 to 3
Outputs:
- grad_rows: bfloat16 [8192, 1024], P(('dp', 'expert'))
- left_stats: float32 [8, 2048, 1024], P('expert', 'dp')
- right_stats: float32 [8, 4096, 2048], P('expert', 'dp')
Inputs may be any that keep to these rules, and one draw needn't show every extreme that they name: Among the rows of one device at most 64 have the same destination, and on some device that many do.
All inputs are finite; a program needn't handle non-finite values.
Results may differ from a plain program's by a relative error of at most 0.001.
Values may be sent and summed in bfloat16 or wider, within the bound.
A program may use at most 128 MiB of HBM per device.

v0:
```python
import jax
import jax.numpy as jnp
from jax import lax
from jax.sharding import PartitionSpec as P

ema_decay = 0.9


def swapped(value, axis, distance):
    mask = 2**distance
    pairs = [(source, source ^ mask) for source in range(lax.axis_size(axis))]
    return lax.ppermute(value, axis, pairs)


def slot_places(dest_column, expert_count, capacity):
    choose = (dest_column[:, None] == jnp.arange(expert_count, dtype=jnp.int32)[None, :]).astype(
        jnp.int32
    )
    before = jnp.cumsum(choose, axis=0) - choose
    slot_rank = jnp.sum(before * choose, axis=1)
    return dest_column * capacity + slot_rank


def local(out_grad, destination, hidden, weight, left_prev, right_prev):
    expert_count = lax.axis_size("expert")
    group_count = lax.axis_size("dp")
    row_count, model_width = out_grad.shape
    slot_count, hidden_width = hidden.shape
    capacity = slot_count // expert_count
    target_slots = slot_places(destination[:, 0], expert_count, capacity)
    outgoing = jnp.zeros((slot_count, model_width), out_grad.dtype).at[target_slots].set(out_grad)
    arrived = lax.all_to_all(
        outgoing.reshape(expert_count, capacity, model_width),
        "expert",
        split_axis=0,
        concat_axis=0,
        tiled=True,
    )
    arrived = arrived.reshape(slot_count, model_width)
    columns = arrived
    slot_grad = lax.dot_general(
        columns,
        lax.all_gather(weight[0], "dp", axis=1, tiled=True),
        (((1,), (1,)), ((), ())),
        preferred_element_type=jnp.float32,
    ).astype(jnp.bfloat16)
    returned = lax.all_to_all(
        slot_grad.reshape(expert_count, capacity, hidden_width),
        "expert",
        split_axis=0,
        concat_axis=0,
        tiled=True,
    )
    grad_rows = returned.reshape(slot_count, hidden_width)[target_slots]
    half_width = model_width // group_count
    block_width = 2 * half_width
    columns_all = lax.all_to_all(arrived, "dp", split_axis=1, concat_axis=0, tiled=True)
    columns = columns_all
    own_piece = lax.dot_general(
        columns,
        lax.all_gather(hidden, "dp", axis=0, tiled=True),
        (((0,), (0,)), ((), ())),
        preferred_element_type=jnp.float32,
    )
    partner = swapped(own_piece.astype(jnp.bfloat16), "dp", 0).astype(own_piece.dtype)
    parity = lax.axis_index("dp") % 2
    upper_half = parity == 0
    first_half = jnp.where(upper_half, own_piece, partner)
    second_half = jnp.where(upper_half, partner, own_piece)
    block_grad = jnp.concatenate([first_half, second_half], axis=0)
    scale_left = 1.0 / (group_count * row_count * block_width)
    scale_right = 1.0 / (group_count * row_count * hidden_width)
    right_gram = (
        lax.dot_general(
            own_piece,
            block_grad,
            (((1,), (1,)), ((), ())),
            precision=lax.Precision.HIGHEST,
            preferred_element_type=jnp.float32,
        )
        * scale_right
    )
    half_hidden = hidden_width // 2
    hidden_cols = lax.dynamic_slice_in_dim(block_grad, parity * half_hidden, half_hidden, 1)
    left_gram = (
        lax.dot_general(
            hidden_cols,
            block_grad,
            (((0,), (0,)), ((), ())),
            precision=lax.Precision.HIGHEST,
            preferred_element_type=jnp.float32,
        )
        * scale_left
    )
    left_stats = ema_decay * left_prev + (1.0 - ema_decay) * left_gram[None]
    right_stats = ema_decay * right_prev + (1.0 - ema_decay) * right_gram[None]
    return (grad_rows, left_stats, right_stats)


def solution(mesh):
    placed = (
        P(("dp", "expert"), None),
        P(("dp", "expert"), None),
        P(("dp", "expert"), None),
        P("expert", None, "dp"),
        P("expert", "dp", None),
        P("expert", "dp", None),
    )
    return jax.shard_map(
        local,
        mesh=mesh,
        in_specs=placed,
        out_specs=(P(("dp", "expert"), None), P("expert", "dp", None), P("expert", "dp", None)),
        check_vma=False,
    )
```

profile of v0, /device:TPU:1, one launch (start us, length us, event | category | flops | bytes accessed | tf_op | source)
XLA Modules:
  0.0 439.9 jit_solution(14873368726343647602)
XLA Ops:
  7.2 0.0 all-gather.4.cloned.1.call-start
  7.2 0.7 all-gather.4.cloned.1.call-update
  7.9 0.7 fusion.15
  8.6 0.6 reduce-window.6
  9.2 0.2 slice_reduce_fusion
  9.4 0.8 fusion.14
  10.2 0.7 compare_select_fusion
  10.9 7.1 %scatter_custom_fusion = bf16[512,4096]{1,0:T(8,128)(2,1)} fusion(s32[256]{0:T(256)S(1)} %bitcast.37, bf16[256,4096]{1,0:T(8,128)(2,1)} %param.6, bf16[]{:T(256)} %constant.14.clone.1), kind=kCustom, calls=%fused_computation.14 | custom fusion | bytes 4194816 | tf_op jit(solution)/shard_map/scatter | solution.py:31
  18.0 5.2 %all-to-all-start = ((bf16[8,64,4096]{2,1,0:T(8,128)(2,1)}), bf16[8,64,4096]{2,1,0:T(8,128)(2,1)}, u32[]{:S(2)}, u32[]{:S(2)}) async-start(bf16[8,64,4096]{2,1,0:T(8,128)(2,1)} %bitcast.34), calls=%async_computation | async-start | bytes 8388608 | tf_op jit(solution)/shard_map/all_to_all | solution.py:32
  23.2 0.0 all-gather.6.cloned.1.call-start
  23.2 0.7 all-gather.6.cloned.1.call-update
  23.9 44.9 %all-to-all-done = bf16[8,64,4096]{2,1,0:T(8,128)(2,1)} async-done(((bf16[8,64,4096]{2,1,0:T(8,128)(2,1)}), bf16[8,64,4096]{2,1,0:T(8,128)(2,1)}, u32[]{:S(2)}, u32[]{:S(2)}) %all-to-all-start) | async-done | bytes 4194336 | tf_op jit(solution)/shard_map/all_to_all | solution.py:32
  68.9 7.8 %all_to_all.22 = bf16[512,4,1024]{2,1,0:T(4,128)(2,1)} reshape(bf16[8,64,4096]{2,1,0:T(8,128)(2,1)} %all-to-all-done) | data formatting | bytes 8388608 | tf_op jit(solution)/shard_map/all_to_all | solution.py:57
  76.7 5.5 %copy.10 = bf16[512,4,1024]{2,0,1:T(8,128)(2,1)} copy(bf16[512,4,1024]{2,1,0:T(4,128)(2,1)} %all_to_all.22) | data formatting | bytes 8388608 | tf_op jit(solution)/shard_map/all_to_all | solution.py:57
  82.2 5.8 %all-to-all-start.2 = ((bf16[512,4,1024]{2,0,1:T(8,128)(2,1)}), bf16[512,4,1024]{2,0,1:T(8,128)(2,1)}, u32[]{:S(2)}, u32[]{:S(2)}) async-start(bf16[512,4,1024]{2,0,1:T(8,128)(2,1)} %copy.10), calls=%async_computation.2 | async-start | bytes 8388608 | tf_op jit(solution)/shard_map/all_to_all | solution.py:57
  88.0 4.2 all-gather.4.cloned.1.call-done
  92.2 194.6 %all-to-all-done.2 = bf16[512,4,1024]{2,0,1:T(8,128)(2,1)} async-done(((bf16[512,4,1024]{2,0,1:T(8,128)(2,1)}), bf16[512,4,1024]{2,0,1:T(8,128)(2,1)}, u32[]{:S(2)}, u32[]{:S(2)}) %all-to-all-start.2) | async-done | bytes 4194336 | tf_op jit(solution)/shard_map/all_to_all | solution.py:57
  286.8 10.7 %fusion.19 = (bf16[1024,1024]{1,0:T(8,128)(2,1)}, f32[1024,1024]{1,0:T(8,128)}) fusion(bf16[2048,1024]{1,0:T(8,128)(2,1)} %bitcast.12, bf16[2048,1024]{1,0:T(8,128)(2,1)} %all-gather.4.cloned.1.call-done), kind=kOutput, calls=%fused_computation.29 | convolution fusion | flops 4296015872 | bytes 14680064 | tf_op jit(solution)/shard_map/dot_general | solution.py:59
  297.5 0.0 collective-permute-start
  297.5 60.1 %collective-permute-done = bf16[1024,1024]{1,0:T(8,128)(2,1)S(1)} collective-permute-done((bf16[1024,1024]{1,0:T(8,128)(2,1)}, bf16[1024,1024]{1,0:T(8,128)(2,1)S(1)}, u32[]{:S(2)}, u32[]{:S(2)}) %collective-permute-start) | collective-permute-done | bytes 2097184 | tf_op jit(solution)/shard_map/ppermute | solution.py:12
  357.6 7.0 %convert_select_fusion.1 = (f32[1024,1024]{1,0:T(8,128)}, f32[1024,1024]{1,0:T(8,128)}) fusion(f32[1024,1024]{1,0:T(8,128)} %get-tuple-element.6, bf16[1024,1024]{1,0:T(8,128)(2,1)S(1)} %collective-permute-done, pred[]{:T(512)S(6)} %eq.38), kind=kLoop, calls=%fused_computation.11 | loop fusion | flops 3145728 | bytes 14680065 | tf_op jit(solution)/shard_map/jit(_where)/select_n | solution.py:68
  364.6 10.2 %fusion.8 = bf16[512,1024]{1,0:T(8,128)(2,1)} fusion(bf16[512,4096]{1,0:T(8,128)(2,1)} %bitcast.7, bf16[1,1024,4096]{2,1,0:T(8,128)(2,1)} %all-gather.6.cloned.1.call-done), kind=kOutput, calls=%fused_computation.16 | convolution fusion | flops 4295491584 | bytes 13631488 | tf_op jit(solution)/shard_map/dot_general | solution.py:41
  374.9 7.8 %all-to-all-start.1 = ((bf16[8,64,1024]{2,1,0:T(8,128)(2,1)}), bf16[8,64,1024]{2,1,0:T(8,128)(2,1)S(1)}, u32[]{:S(2)}, u32[]{:S(2)}) async-start(bf16[8,64,1024]{2,1,0:T(8,128)(2,1)} %bitcast.9), calls=%async_computation.1 | async-start | bytes 2097152 | tf_op jit(solution)/shard_map/all_to_all | solution.py:47
  382.7 0.0 copy-start
  382.7 0.0 copy-start.1
  382.7 0.0 copy-start.2
  382.7 33.1 %bitcast_add_fusion = f32[1,1024,2048]{2,1,0:T(8,128)} fusion(f32[1,1024,2048]{2,1,0:T(8,128)} %param.11, f32[1024,1024]{1,0:T(8,128)} %get-tuple-element.6, f32[1024,1024]{1,0:T(8,128)} %get-tuple-element.4, f32[1024,1024]{1,0:T(8,128)} %get-tuple-element.3), kind=kOutput, calls=%fused_computation.5 | convolution fusion | flops 25778192384 | bytes 29360128 | tf_op jit(solution)/shard_map/dot_general | solution.py:74
  415.8 0.0 copy-done
  415.8 0.0 copy-done.1
  415.8 15.1 %bitcast_add_fusion.1 = f32[1,512,1024]{2,1,0:T(8,128)} fusion(f32[1,512,1024]{2,1,0:T(8,128)S(1)} %copy-done.2, f32[1024,1024]{1,0:T(8,128)S(1)} %copy-done.1, f32[1024,1024]{1,0:T(8,128)S(1)} %copy-done, s32[]{:T(128)S(6)} %select_n.32), kind=kOutput, calls=%fused_computation.13 | convolution fusion | flops 12889620480 | bytes 20971524 | tf_op jit(solution)/shard_map/dot_general | solution.py:86
  430.9 0.0 all-to-all-done.1
  430.9 2.0 gather_fusion
  (5 shorter events, 0.1 us)
Async XLA Ops:
  7.2 85.1 %all-gather.4.cloned.1.call-start = ((), (), s32[]{:S(2)}) async-start(), calls=%async_computation.3 | async-start | bytes 5242880 | tf_op jit(solution)/shard_map/all_gather | solution.py:61
  18.0 50.9 %all-to-all-start = ((bf16[8,64,4096]{2,1,0:T(8,128)(2,1)}), bf16[8,64,4096]{2,1,0:T(8,128)(2,1)}, u32[]{:S(2)}, u32[]{:S(2)}) async-start(bf16[8,64,4096]{2,1,0:T(8,128)(2,1)} %bitcast.34), calls=%async_computation | async-start | bytes 8388608 | tf_op jit(solution)/shard_map/all_to_all | solution.py:32
  23.2 341.4 %all-gather.6.cloned.1.call-start = ((), (), s32[]{:S(2)}) async-start(), calls=%async_computation.4 | async-start | bytes 10485760 | tf_op jit(solution)/shard_map/all_gather | solution.py:43
  82.2 204.6 %all-to-all-start.2 = ((bf16[512,4,1024]{2,0,1:T(8,128)(2,1)}), bf16[512,4,1024]{2,0,1:T(8,128)(2,1)}, u32[]{:S(2)}, u32[]{:S(2)}) async-start(bf16[512,4,1024]{2,0,1:T(8,128)(2,1)} %copy.10), calls=%async_computation.2 | async-start | bytes 8388608 | tf_op jit(solution)/shard_map/all_to_all | solution.py:57
  297.5 60.1 %collective-permute-start = (bf16[1024,1024]{1,0:T(8,128)(2,1)}, bf16[1024,1024]{1,0:T(8,128)(2,1)S(1)}, u32[]{:S(2)}, u32[]{:S(2)}) collective-permute-start(bf16[1024,1024]{1,0:T(8,128)(2,1)} %get-tuple-element.5), channel_id=1, source_target_pairs={{0,8},{8,0},{16,24},{24,16},{1,9},{9,1},{17,25},{25,17},{2,10},{10... | collective-permute-start | bytes 6291464 | tf_op jit(solution)/shard_map/ppermute | solution.py:12
  374.9 56.1 %all-to-all-start.1 = ((bf16[8,64,1024]{2,1,0:T(8,128)(2,1)}), bf16[8,64,1024]{2,1,0:T(8,128)(2,1)S(1)}, u32[]{:S(2)}, u32[]{:S(2)}) async-start(bf16[8,64,1024]{2,1,0:T(8,128)(2,1)} %bitcast.9), calls=%async_computation.1 | async-start | bytes 2097152 | tf_op jit(solution)/shard_map/all_to_all | solution.py:47
  382.7 33.1 %copy-start = (f32[1024,1024]{1,0:T(8,128)S(1)}, f32[1024,1024]{1,0:T(8,128)}, u32[]{:S(2)}) copy-start(f32[1024,1024]{1,0:T(8,128)} %get-tuple-element.3) | copy-start | bytes 12582916
  382.7 33.1 %copy-start.1 = (f32[1024,1024]{1,0:T(8,128)S(1)}, f32[1024,1024]{1,0:T(8,128)}, u32[]{:S(2)}) copy-start(f32[1024,1024]{1,0:T(8,128)} %get-tuple-element.4) | copy-start | bytes 12582916
  382.7 33.1 %copy-start.2 = (f32[1,512,1024]{2,1,0:T(8,128)S(1)}, f32[1,512,1024]{2,1,0:T(8,128)}, u32[]{:S(2)}) copy-start(f32[1,512,1024]{2,1,0:T(8,128)} %param.10) | copy-start | bytes 6291460
Sparse Core Ops, SparseCore 0:
  9.5 82.6 all-gather.3
  93.8 223.5 all-gather.5
where the time goes:
time: 446 us; the launch traced here: 440 us
  waiting for transfers between devices  305 us (68%)
  matrix products  69.1 us (15%)
  local copies, waits for them, and re-layouts  22.6 us (5%)
  starting transfers between devices  18.9 us (4%)
  between operations  14.3 us (3%)
  other arithmetic  9.75 us (2%)
    all_to_all x1, waiting for transfers between devices, local(): lax.all_to_all(arrived, 'dp', split_axis=1, concat_axis=0, tiled=True)  195 us
    ppermute x1, waiting for transfers between devices, swapped(): return lax.ppermute(value, axis, pairs)  60.1 us
    all_to_all x1, waiting for transfers between devices, local(): lax.all_to_all(outgoing.reshape(expert_count, capacity, model_width), 'ex...  44.9 us
    dot_general x1, matrix products, local(): lax.dot_general(own_piece, block_grad, (((1,), (1,)), ((), ())), precisio...  33.1 us
    dot_general x1, matrix products, local(): lax.dot_general(hidden_cols, block_grad, (((0,), (0,)), ((), ())), precis...  15.1 us
    all_to_all x2, local copies, waits for them, and re-layouts, local(): lax.all_to_all(arrived, 'dp', split_axis=1, concat_axis=0, tiled=True)  13.3 us
    dot_general x1, matrix products, local(): lax.dot_general(columns, lax.all_gather(hidden, 'dp', axis=0, tiled=True)...  10.7 us
    dot_general x1, matrix products, local(): lax.dot_general(columns, lax.all_gather(weight[0], 'dp', axis=1, tiled=Tr...  10.2 us
  transfers between devices with their start and end apart: 6, of which 4 were waited for; matrix products, arithmetic and copies ran while one was open for 19% of the time, Pallas kernels for 0%

commit v1 on v0

v1 whole, which is shorter than its diff:
```python
import functools

import jax
import jax.numpy as jnp
from jax import lax
from jax.experimental import pallas as pl
from jax.experimental.pallas import tpu as pltpu
from jax.sharding import PartitionSpec as P

MESH = pl.DeviceIdType.MESH
ema_decay = 0.9


def swapped(value, axis, distance):
    mask = 2**distance
    pairs = [(source, source ^ mask) for source in range(lax.axis_size(axis))]
    return lax.ppermute(value, axis, pairs)


def slot_choice(dest, expert_count, capacity):
    row_count = dest.shape[-1]
    choose = dest[..., None] == jnp.arange(expert_count, dtype=jnp.int32)
    earlier = jnp.tril(jnp.ones((row_count, row_count), jnp.bfloat16), -1)
    before = jnp.einsum(
        "rq,...qe->...re", earlier, choose.astype(jnp.bfloat16), preferred_element_type=jnp.float32
    )
    rank = jnp.sum(jnp.where(choose, before, 0.0), axis=-1).astype(jnp.int32)
    slots = dest * capacity + rank
    ids = jnp.arange(expert_count * capacity, dtype=jnp.int32)
    return slots, (ids[:, None] == slots[..., None, :]).astype(jnp.bfloat16)


def greet(peers):
    barrier = pltpu.get_barrier_semaphore()
    for peer in peers:
        pl.semaphore_signal(barrier, inc=1, device_id=peer, device_id_type=MESH)
    pl.semaphore_wait(barrier, len(peers))


def send(source, target, sends, receives, at, peer):
    copy = pltpu.make_async_remote_copy(
        src_ref=source,
        dst_ref=target,
        send_sem=sends.at[at],
        recv_sem=receives.at[at],
        device_id=peer,
        device_id_type=MESH,
    )
    copy.start()
    return copy


def first_kernel(
    groups, experts, rows, dest, slots, columns, dest_all, arrived, sends, receives, own
):
    g, e = lax.axis_index("dp"), lax.axis_index("expert")
    width = rows.shape[1] // groups
    others = [lax.rem(g + k, groups) for k in range(1, groups)]
    mates = [lax.rem(e + k, experts) for k in range(1, experts)]
    greet([{"dp": o} for o in others] + [{"expert": m} for m in mates])
    copies = []
    for o in others:
        copies.append(send(dest, dest_all.at[g], sends, receives, len(copies), {"dp": o}))
    for o in others:
        part = rows.at[:, pl.ds(pl.multiple_of(o * width, width), width)]
        copies.append(send(part, columns.at[g], sends, receives, len(copies), {"dp": o}))
    for m in mates:
        copies.append(send(slots.at[m], arrived.at[e], sends, receives, len(copies), {"expert": m}))
    mine = rows.at[:, pl.ds(pl.multiple_of(g * width, width), width)]
    local_copies = [
        pltpu.make_async_copy(dest, dest_all.at[g], own.at[0]),
        pltpu.make_async_copy(mine, columns.at[g], own.at[1]),
        pltpu.make_async_copy(slots.at[e], arrived.at[e], own.at[2]),
    ]
    for copy in local_copies:
        copy.start()
    for copy in copies:
        copy.wait()
    for copy in local_copies:
        copy.wait()


def first_exchange(rows, dest, slots, groups, experts):
    row_count, model_width = rows.shape
    count = 2 * (groups - 1) + experts - 1
    anywhere = pl.BlockSpec(memory_space=pl.ANY)
    return pl.pallas_call(
        functools.partial(first_kernel, groups, experts),
        out_shape=(
            jax.ShapeDtypeStruct((groups, row_count, model_width // groups), rows.dtype),
            jax.ShapeDtypeStruct((groups,) + dest.shape, dest.dtype),
            jax.ShapeDtypeStruct(slots.shape, slots.dtype),
        ),
        in_specs=[anywhere] * 3,
        out_specs=(anywhere,) * 3,
        scratch_shapes=[
            pltpu.SemaphoreType.DMA((count,)),
            pltpu.SemaphoreType.DMA((count,)),
            pltpu.SemaphoreType.DMA((3,)),
        ],
        compiler_params=pltpu.CompilerParams(collective_id=1, has_side_effects=True),
        name="first_exchange",
    )(rows, dest, slots)


def second_kernel(experts, slots, arrived, sends, receives, own):
    e = lax.axis_index("expert")
    mates = [lax.rem(e + k, experts) for k in range(1, experts)]
    greet([{"expert": m} for m in mates])
    copies = []
    for m in mates:
        copies.append(
            send(slots.at[:, m], arrived.at[:, e], sends, receives, len(copies), {"expert": m})
        )
    local_copy = pltpu.make_async_copy(slots.at[:, e], arrived.at[:, e], own)
    local_copy.start()
    for copy in copies:
        copy.wait()
    local_copy.wait()


def second_exchange(slots, experts):
    anywhere = pl.BlockSpec(memory_space=pl.ANY)
    return pl.pallas_call(
        functools.partial(second_kernel, experts),
        out_shape=jax.ShapeDtypeStruct(slots.shape, slots.dtype),
        in_specs=[anywhere],
        out_specs=anywhere,
        scratch_shapes=[
            pltpu.SemaphoreType.DMA((experts - 1,)),
            pltpu.SemaphoreType.DMA((experts - 1,)),
            pltpu.SemaphoreType.DMA,
        ],
        compiler_params=pltpu.CompilerParams(collective_id=2, has_side_effects=True),
        name="second_exchange",
    )(slots)


def local(out_grad, destination, hidden, weight, left_prev, right_prev):
    expert_count = lax.axis_size("expert")
    group_count = lax.axis_size("dp")
    row_count, model_width = out_grad.shape
    slot_count, hidden_width = hidden.shape
    capacity = slot_count // expert_count
    half_width = model_width // group_count
    block_width = 2 * half_width

    hidden_all = lax.all_gather(hidden, "dp", axis=0, tiled=True)
    target_slots, own_choice = slot_choice(destination[:, 0], expert_count, capacity)
    outgoing = jnp.dot(own_choice, out_grad, preferred_element_type=jnp.float32).astype(
        out_grad.dtype
    )
    column_rows, dest_all, arrived = first_exchange(
        out_grad,
        destination.reshape(row_count // 128, 128),
        outgoing.reshape(expert_count, capacity, model_width),
        group_count,
        expert_count,
    )
    arrived = arrived.reshape(slot_count, model_width)
    weight_late, column_rows = lax.optimization_barrier((weight[0], column_rows))
    weight_all = lax.all_gather(weight_late, "dp", axis=0)

    _, all_choice = slot_choice(dest_all.reshape(group_count, row_count), expert_count, capacity)
    column_slots = lax.dot_general(
        all_choice,
        column_rows,
        (((2,), (1,)), ((0,), (0,))),
        preferred_element_type=jnp.float32,
    ).astype(out_grad.dtype)
    columns = second_exchange(
        column_slots.reshape(group_count, expert_count, capacity, half_width), expert_count
    )
    hidden_slots = hidden_all
    own_piece = lax.dot_general(
        columns.reshape(-1, half_width),
        hidden_slots,
        (((0,), (0,)), ((), ())),
        preferred_element_type=jnp.float32,
    ).astype(jnp.bfloat16)
    partner = swapped(own_piece, "dp", 0)
    parity = lax.axis_index("dp") % 2
    upper_half = parity == 0
    first_half = jnp.where(upper_half, own_piece, partner)
    second_half = jnp.where(upper_half, partner, own_piece)
    block_grad = jnp.concatenate([first_half, second_half], axis=0)
    scale_left = 1.0 / (group_count * row_count * block_width)
    scale_right = 1.0 / (group_count * row_count * hidden_width)
    right_gram = (
        lax.dot_general(
            own_piece,
            block_grad,
            (((1,), (1,)), ((), ())),
            preferred_element_type=jnp.float32,
        )
        * scale_right
    )
    half_hidden = hidden_width // 2
    hidden_cols = lax.dynamic_slice_in_dim(block_grad, parity * half_hidden, half_hidden, 1)
    left_gram = (
        lax.dot_general(
            hidden_cols,
            block_grad,
            (((0,), (0,)), ((), ())),
            preferred_element_type=jnp.float32,
        )
        * scale_left
    )
    left_stats = ema_decay * left_prev + (1.0 - ema_decay) * left_gram[None]
    right_stats = ema_decay * right_prev + (1.0 - ema_decay) * right_gram[None]

    arrived, _, _ = lax.optimization_barrier((arrived, left_stats, right_stats))
    slot_grad = sum(
        lax.dot_general(
            arrived[:, part * half_width : (part + 1) * half_width],
            weight_all[part],
            (((1,), (1,)), ((), ())),
            preferred_element_type=jnp.float32,
        )
        for part in range(group_count)
    ).astype(jnp.bfloat16)
    returned = lax.all_to_all(
        slot_grad.reshape(expert_count, capacity, hidden_width),
        "expert",
        split_axis=0,
        concat_axis=0,
        tiled=True,
    )
    grad_rows = returned.reshape(slot_count, hidden_width)[target_slots]
    return (grad_rows, left_stats, right_stats)


def solution(mesh):
    placed = (
        P(("dp", "expert"), None),
        P(("dp", "expert"), None),
        P(("dp", "expert"), None),
        P("expert", None, "dp"),
        P("expert", "dp", None),
        P("expert", "dp", None),
    )
    return jax.shard_map(
        local,
        mesh=mesh,
        in_specs=placed,
        out_specs=(P(("dp", "expert"), None), P("expert", "dp", None), P("expert", "dp", None)),
        check_vma=False,
    )
```

time: 446 us -> 377 us (0.85)
  waiting for transfers between devices: 305 us -> 154 us
  Pallas kernels: 0 us -> 122 us
  matrix products: 69.1 us -> 40.4 us
  local copies, waits for them, and re-layouts: 22.6 us -> 4.28 us
  starting transfers between devices: 18.9 us -> 35.8 us
  other arithmetic: 9.75 us -> 2.73 us
    all_to_all x2 -> x0, waiting for transfers between devices: 239 us -> none  [the longest x1 195 us: local(): lax.all_to_all(arrived, 'dp', split_axis=1, concat_axis=0, tiled=True)]
    pallas_call x0 -> x2, Pallas kernels: none -> 122 us  [the longest x1 69.4 us: first_exchange(): pl.pallas_call(functools.partial(first_kernel, groups, experts), out_shap...]
    ppermute x1, waiting for transfers between devices: 60.1 us -> 142 us  [swapped(): return lax.ppermute(value, axis, pairs)]
    ppermute x1, starting transfers between devices: 0.01 us -> 31.9 us  [swapped(): return lax.ppermute(value, axis, pairs)]
    dot_general x4 -> x11, matrix products: 69.1 us -> 40.4 us  [the longest x4 9.64 us: local(): lax.dot_general(arrived[:, part * half_width:(part + 1) * half_width], we...]
    all_to_all x2 -> x0, local copies, waits for them, and re-layouts: 13.3 us -> none  [local(): lax.all_to_all(arrived, 'dp', split_axis=1, concat_axis=0, tiled=True)]
    all_to_all x1, waiting for transfers between devices: 0.01 us -> 11.9 us  [local(): lax.all_to_all(slot_grad.reshape(expert_count, capacity, hidden_width), '...]
    all_to_all x2 -> x0, starting transfers between devices: 11 us -> none  [the longest x1 5.83 us: local(): lax.all_to_all(arrived, 'dp', split_axis=1, concat_axis=0, tiled=True)]
  transfers between devices with their start and end apart: 6 -> 4, of which waited for: 4 -> 2; matrix products, arithmetic and copies ran while one was open for 19% -> 9% of each run, Pallas kernels for 0% -> 33%
where the time goes in v1:
time: 377 us; the launch traced here: 373 us
  waiting for transfers between devices  154 us (41%)
  Pallas kernels  122 us (32%)
  matrix products  40.4 us (11%)
  starting transfers between devices  35.8 us (9%)
  between operations  14.2 us (4%)
  local copies, waits for them, and re-layouts  4.28 us (1%)
    ppermute x1, waiting for transfers between devices, swapped(): return lax.ppermute(value, axis, pairs)  142 us
    pallas_call x1, Pallas kernels, first_exchange(): pl.pallas_call(functools.partial(first_kernel, groups, experts), out_shap...  69.4 us
    pallas_call x1, Pallas kernels, second_exchange(): pl.pallas_call(functools.partial(second_kernel, experts), out_shape=jax.S...  52.2 us
    ppermute x1, starting transfers between devices, swapped(): return lax.ppermute(value, axis, pairs)  31.9 us
    all_to_all x1, waiting for transfers between devices, local(): lax.all_to_all(slot_grad.reshape(expert_count, capacity, hidden_width), '...  11.9 us
    dot_general x4, matrix products, local(): lax.dot_general(arrived[:, part * half_width:(part + 1) * half_width], we...  9.64 us
    dot_general x1, matrix products, local(): lax.dot_general(columns.reshape(-1, half_width), hidden_slots, (((0,), (0...  9.13 us
    dot_general x1, matrix products, local(): lax.dot_general(own_piece, block_grad, (((1,), (1,)), ((), ())), preferre...  8.47 us
  transfers between devices with their start and end apart: 4, of which 2 were waited for; matrix products, arithmetic and copies ran while one was open for 9% of the time, Pallas kernels for 33%

profile of v1, /device:TPU:1, one launch (start us, length us, event | category | flops | bytes accessed | tf_op | source)
XLA Modules:
  0.0 373.1 jit_solution(14881759573214123180)
XLA Ops:
  7.2 0.0 all-gather.4.cloned.1.call-start
  7.2 0.7 all-gather.4.cloned.1.call-update
  7.9 0.0 all-gather.6.cloned.1.call-start
  8.0 1.0 fusion.15
  9.0 0.7 multiply_add_fusion
  9.7 4.9 %convolution_convert_fusion = bf16[512,4096]{1,0:T(8,128)(2,1)} fusion(bf16[256,4096]{1,0:T(8,128)(2,1)} %rows.1, s32[256]{0:T(256)S(1)} %multiply_add_fusion), kind=kOutput, calls=%fused_computation.2 | convolution fusion | flops 1075970048 | bytes 6292480 | tf_op jit(solution)/shard_map/dot_general | solution.py:150
  14.5 69.4 %first_exchange.1 = (bf16[4,256,1024]{2,1,0:T(8,128)(2,1)}, s32[4,2,128]{2,1,0:T(2,128)}, bf16[8,64,4096]{2,1,0:T(8,128)(2,1)}) custom-call(bf16[256,4096]{1,0:T(8,128)(2,1)} %rows.1, s32[2,128]{1,0:T(2,128)} %bitcast.48, bf16[8,64,4096]{2,1,0:T(8,128)(2,1)} %bitcast.36), custom_call_target="tpu_custom_call" | custom-call | tf_op jit(solution)/shard_map/first_exchange/pallas_call | solution.py:87
  83.9 0.0 all-gather.6.cloned.1.call-update
  83.9 0.6 copy-done.3
  84.6 0.3 fusion.14
  84.9 0.7 copy-done
  85.5 3.3 convolution_convert_fusion.1
  88.8 52.2 %second_exchange.1 = bf16[4,8,64,1024]{3,2,1,0:T(8,128)(2,1)} custom-call(bf16[4,8,64,1024]{3,2,1,0:T(8,128)(2,1)} %bitcast.37), custom_call_target="tpu_custom_call" | custom-call | tf_op jit(solution)/shard_map/second_exchange/pallas_call | solution.py:124
  141.0 0.0 all-gather.4.cloned.1.call-done
  141.0 9.1 %convolution_convert_fusion.2 = bf16[1024,1024]{1,0:T(8,128)(2,1)S(1)} fusion(bf16[2048,1024]{1,0:T(8,128)(2,1)} %bitcast.38, bf16[2048,1024]{1,0:T(8,128)(2,1)} %all-gather.4.cloned.1.call-done), kind=kOutput, calls=%fused_computation.22 | convolution fusion | flops 4296015872 | bytes 10485760 | tf_op jit(solution)/shard_map/dot_general | solution.py:175
  150.2 31.9 %collective-permute-start = (bf16[1024,1024]{1,0:T(8,128)(2,1)S(1)}, bf16[1024,1024]{1,0:T(8,128)(2,1)}, u32[]{:S(2)}, u32[]{:S(2)}) collective-permute-start(bf16[1024,1024]{1,0:T(8,128)(2,1)S(1)} %convolution_convert_fusion.2), channel_id=1, source_target_pairs={{0,8},{8,0},{16,24},{24,16},{1,9},{9,1},{17,25},{25,17},{2,10},{10... | collective-permute-start | bytes 6291464 | tf_op jit(solution)/shard_map/ppermute | solution.py:17
  182.1 141.6 %collective-permute-done = bf16[1024,1024]{1,0:T(8,128)(2,1)} collective-permute-done((bf16[1024,1024]{1,0:T(8,128)(2,1)S(1)}, bf16[1024,1024]{1,0:T(8,128)(2,1)}, u32[]{:S(2)}, u32[]{:S(2)}) %collective-permute-start) | collective-permute-done | bytes 2097184 | tf_op jit(solution)/shard_map/ppermute | solution.py:17
  323.7 2.0 broadcast_select_fusion.1
  325.7 0.0 copy-done.5
  325.7 0.0 slice-start.1
  325.7 3.7 bitcast_add_fusion.1
  329.5 8.5 %bitcast_add_fusion = f32[1,1024,2048]{2,1,0:T(8,128)} fusion(f32[1,1024,2048]{2,1,0:T(8,128)S(1)} %bitcast.53, bf16[1024,1024]{1,0:T(8,128)(2,1)S(1)} %convolution_convert_fusion.2, bf16[1024,1024]{1,0:T(8,128)(2,1)S(1)} %get-tuple-element.16, bf16[1024,1024]{1,0:T(8,128)(2,1)S(1)} %get-tuple-element.15), kind=kOutput, calls=%fused_computation.1 | convolution fusion | flops 4309647360 | bytes 23068672 | tf_op jit(solution)/shard_map/dot_general | solution.py:190
  338.0 3.3 fusion.7
  341.3 1.0 copy-done.1
  342.3 2.7 fusion.5
  345.0 0.0 copy-done.2
  345.0 1.3 fusion.3
  346.3 2.3 add_convert_fusion
  348.6 3.8 %all-to-all-start = ((bf16[8,64,1024]{2,1,0:T(8,128)(2,1)}), bf16[8,64,1024]{2,1,0:T(8,128)(2,1)S(1)}, u32[]{:S(2)}, u32[]{:S(2)}) async-start(bf16[8,64,1024]{2,1,0:T(8,128)(2,1)} %bitcast.11), calls=%async_computation | async-start | bytes 2097152 | tf_op jit(solution)/shard_map/all_to_all | solution.py:222
  352.4 0.0 copy-done.4
  352.4 11.9 %all-to-all-done = bf16[8,64,1024]{2,1,0:T(8,128)(2,1)S(1)} async-done(((bf16[8,64,1024]{2,1,0:T(8,128)(2,1)}), bf16[8,64,1024]{2,1,0:T(8,128)(2,1)S(1)}, u32[]{:S(2)}, u32[]{:S(2)}) %all-to-all-start) | async-done | bytes 1048608 | tf_op jit(solution)/shard_map/all_to_all | solution.py:222
  364.3 2.0 gather_fusion
  (17 shorter events, 0.0 us)
Async XLA Ops:
  7.2 133.9 %all-gather.4.cloned.1.call-start = ((), (), s32[]{:S(2)}) async-start(), calls=%async_computation.1 | async-start | bytes 5242880 | tf_op jit(solution)/shard_map/all_gather | solution.py:148
  7.9 330.1 %all-gather.6.cloned.1.call-start = ((), (), s32[]{:S(2)}) async-start(), calls=%async_computation.2 | async-start | bytes 10485760 | tf_op jit(solution)/shard_map/all_gather | solution.py:162
  83.9 0.7 copy-start.3
  83.9 1.6 copy-start
  150.2 173.5 %collective-permute-start = (bf16[1024,1024]{1,0:T(8,128)(2,1)S(1)}, bf16[1024,1024]{1,0:T(8,128)(2,1)}, u32[]{:S(2)}, u32[]{:S(2)}) collective-permute-start(bf16[1024,1024]{1,0:T(8,128)(2,1)S(1)} %convolution_convert_fusion.2), channel_id=1, source_target_pairs={{0,8},{8,0},{16,24},{24,16},{1,9},{9,1},{17,25},{25,17},{2,10},{10... | collective-permute-start | bytes 6291464 | tf_op jit(solution)/shard_map/ppermute | solution.py:17
  182.1 143.7 %copy-start.5 = (f32[1,512,1024]{2,1,0:T(8,128)S(1)}, f32[1,512,1024]{2,1,0:T(8,128)}, u32[]{:S(2)}) copy-start(f32[1,512,1024]{2,1,0:T(8,128)} %param.10) | copy-start | bytes 6291460
  323.7 5.8 %slice-start = ((s8[8388608]{0:T(1024)(128)(4,1)}), s8[4194304]{0:T(1024)(128)(4,1)S(1)}, s32[]{:S(2)}) async-start(s8[8388608]{0:T(1024)(128)(4,1)} %bitcast.52), calls=%async_computation.3 | async-start | bytes 8388608
  325.7 3.7 %slice-start.1 = ((s8[8388608]{0:T(1024)(128)(4,1)}), s8[4194304]{0:T(1024)(128)(4,1)S(1)}, s32[]{:S(2)}) async-start(s8[8388608]{0:T(1024)(128)(4,1)} %bitcast.52), calls=%async_computation.4 | async-start | bytes 8388608
  337.9 4.3 %copy-start.1 = (bf16[4096,1024]{1,0:T(8,128)(2,1)S(1)}, bf16[4096,1024]{1,0:T(8,128)(2,1)}, u32[]{:S(2)}) copy-start(bf16[4096,1024]{1,0:T(8,128)(2,1)} %all-gather.6.cloned.1.call-done) | copy-start | bytes 25165828
  342.3 2.7 copy-start.2
  348.6 3.8 %copy-start.4 = (s32[256,1]{0,1:T(1,128)S(1)}, s32[256,1]{0,1:T(1,128)}, u32[]{:S(2)}) copy-start(s32[256,1]{0,1:T(1,128)} %param.7) | copy-start | bytes 3076
  348.6 15.7 %all-to-all-start = ((bf16[8,64,1024]{2,1,0:T(8,128)(2,1)}), bf16[8,64,1024]{2,1,0:T(8,128)(2,1)S(1)}, u32[]{:S(2)}, u32[]{:S(2)}) async-start(bf16[8,64,1024]{2,1,0:T(8,128)(2,1)} %bitcast.11), calls=%async_computation | async-start | bytes 2097152 | tf_op jit(solution)/shard_map/all_to_all | solution.py:222
Sparse Core Ops, SparseCore 0:
  9.5 124.9 all-gather.3
  136.1 190.4 all-gather.5

commit v2 on v1

--- a/solution.py
+++ b/solution.py
@@ -119,7 +119,7 @@
     local_copy.wait()
 
 
-def second_exchange(slots, experts):
+def expert_exchange(slots, experts, number, weight=32):
     anywhere = pl.BlockSpec(memory_space=pl.ANY)
     return pl.pallas_call(
         functools.partial(second_kernel, experts),
@@ -131,8 +131,10 @@
             pltpu.SemaphoreType.DMA((experts - 1,)),
             pltpu.SemaphoreType.DMA,
         ],
-        compiler_params=pltpu.CompilerParams(collective_id=2, has_side_effects=True),
-        name="second_exchange",
+        cost_estimate=pl.CostEstimate(
+            flops=0, bytes_accessed=weight * slots.size * slots.dtype.itemsize, transcendentals=0
+        ),
+        compiler_params=pltpu.CompilerParams(collective_id=number, has_side_effects=True),
     )(slots)
 
 
@@ -158,8 +160,20 @@
         expert_count,
     )
     arrived = arrived.reshape(slot_count, model_width)
-    weight_late, column_rows = lax.optimization_barrier((weight[0], column_rows))
-    weight_all = lax.all_gather(weight_late, "dp", axis=0)
+    group = lax.axis_index("dp")
+    helped = group_count == 4
+    if helped:
+        inward, across, outward = [(0, 1), (3, 2)], [(1, 2), (2, 1)], [(1, 0), (2, 3)]
+        weight_in = lax.ppermute(weight[0], "dp", inward)
+        weight_late, weight_mid, rows_late, column_rows = lax.optimization_barrier(
+            (weight[0], weight_in, out_grad, column_rows)
+        )
+        weight_across = lax.ppermute(weight_late, "dp", across)
+        weight_far = lax.ppermute(weight_mid, "dp", across)
+        rows_in = lax.ppermute(rows_late, "dp", inward)
+    else:
+        weight_late, column_rows = lax.optimization_barrier((weight[0], column_rows))
+        weight_all = lax.all_gather(weight_late, "dp", axis=0)
 
     _, all_choice = slot_choice(dest_all.reshape(group_count, row_count), expert_count, capacity)
     column_slots = lax.dot_general(
@@ -168,8 +182,11 @@
         (((2,), (1,)), ((0,), (0,))),
         preferred_element_type=jnp.float32,
     ).astype(out_grad.dtype)
-    columns = second_exchange(
-        column_slots.reshape(group_count, expert_count, capacity, half_width), expert_count
+    columns = expert_exchange(
+        column_slots.reshape(group_count, expert_count, capacity, half_width),
+        expert_count,
+        2,
+        1,
     )
     hidden_slots = hidden_all
     own_piece = lax.dot_general(
@@ -209,22 +226,57 @@
     left_stats = ema_decay * left_prev + (1.0 - ema_decay) * left_gram[None]
     right_stats = ema_decay * right_prev + (1.0 - ema_decay) * right_gram[None]
 
+    def against(values, part, weight_part):
+        taken = lax.dynamic_slice_in_dim(values, part * half_width, half_width, 1)
+        return lax.dot_general(
+            taken, weight_part, (((1,), (1,)), ((), ())), preferred_element_type=jnp.float32
+        )
+
+    if helped:
+        pair = group ^ 1
+        arrived, rows_in, _ = lax.optimization_barrier((arrived, rows_in, own_piece))
+        pair_dest = lax.dynamic_index_in_dim(dest_all, pair, 0, keepdims=False)
+        pair_slots, pair_choice = slot_choice(
+            pair_dest.reshape(row_count), expert_count, capacity
+        )
+        pair_outgoing = jnp.dot(
+            pair_choice, rows_in, preferred_element_type=jnp.float32
+        ).astype(out_grad.dtype)
+        pair_arrived = expert_exchange(
+            pair_outgoing.reshape(1, expert_count, capacity, model_width), expert_count, 3
+        ).reshape(slot_count, model_width)
+        far = group_count - 1 - group
+        weight_across, weight_far, pair_arrived, _ = lax.optimization_barrier(
+            (weight_across, weight_far, pair_arrived, partner)
+        )
+        held = (
+            (group, weight_late),
+            (pair, weight_in),
+            (far, weight_across),
+            (far ^ 1, weight_far),
+        )
+        slot_grads = jnp.stack(
+            [
+                sum(against(values, part, piece) for part, piece in held).astype(jnp.bfloat16)
+                for values in (arrived, pair_arrived)
+            ]
+        )
+        returned = expert_exchange(
+            slot_grads.reshape(2, expert_count, capacity, hidden_width), expert_count, 4
+        ).reshape(2, slot_count, hidden_width)
+        own_rows = returned[0][target_slots]
+        pair_rows = lax.ppermute(returned[1][pair_slots], "dp", outward)
+        own_rows, _, _ = lax.optimization_barrier((own_rows, left_stats, right_stats))
+        inner = (group == 1) | (group == 2)
+        grad_rows = jnp.where(inner, own_rows, pair_rows)
+        return (grad_rows, left_stats, right_stats)
+
     arrived, _, _ = lax.optimization_barrier((arrived, left_stats, right_stats))
-    slot_grad = sum(
-        lax.dot_general(
-            arrived[:, part * half_width : (part + 1) * half_width],
-            weight_all[part],
-            (((1,), (1,)), ((), ())),
-            preferred_element_type=jnp.float32,
-        )
-        for part in range(group_count)
-    ).astype(jnp.bfloat16)
-    returned = lax.all_to_all(
-        slot_grad.reshape(expert_count, capacity, hidden_width),
-        "expert",
-        split_axis=0,
-        concat_axis=0,
-        tiled=True,
+    slot_grad = sum(against(arrived, part, weight_all[part]) for part in range(group_count)).astype(
+        jnp.bfloat16
+    )
+    returned = expert_exchange(
+        slot_grad.reshape(1, expert_count, capacity, hidden_width), expert_count, 4
     )
     grad_rows = returned.reshape(slot_count, hidden_width)[target_slots]
     return (grad_rows, left_stats, right_stats)
@@ -239,6 +291,7 @@
         P("expert", "dp", None),
         P("expert", "dp", None),
     )
+
     return jax.shard_map(
         local,
         mesh=mesh,

time: 377 us -> 398 us (1.056)
  Pallas kernels: 122 us -> 265 us
  waiting for transfers between devices: 154 us -> 28.1 us
  starting transfers between devices: 35.8 us -> 14.3 us
  matrix products: 40.4 us -> 59.8 us
  other arithmetic: 2.73 us -> 6.92 us
    ppermute x1, waiting for transfers between devices: 142 us -> 0.01 us  [swapped(): return lax.ppermute(value, axis, pairs)]
    pallas_call x1 -> x3, Pallas kernels: 52.2 us -> 125 us  [expert_exchange(): pl.pallas_call(functools.partial(second_kernel, experts), out_shape=jax.S...]
    pallas_call x1, Pallas kernels: 69.4 us -> 139 us  [first_exchange(): pl.pallas_call(functools.partial(first_kernel, groups, experts), out_shap...]
    ppermute x1, starting transfers between devices: 31.9 us -> 2.31 us  [swapped(): return lax.ppermute(value, axis, pairs)]
    ppermute x0 -> x5, waiting for transfers between devices: none -> 27.5 us  [the longest x1 27.4 us: local(): rows_in = lax.ppermute(rows_late, 'dp', inward)]
    dot_general x4 -> x9, matrix products: 9.64 us -> 23.2 us  [the longest x8 18.4 us: against(): lax.dot_general(taken, weight_part, (((1,), (1,)), ((), ())), preferred_e...]
    ppermute x0 -> x5, starting transfers between devices: none -> 12 us  [the longest x1 4.15 us: local(): weight_in = lax.ppermute(weight[0], 'dp', inward)]
    all_to_all x1 -> x0, waiting for transfers between devices: 11.9 us -> none  [local(): lax.all_to_all(slot_grad.reshape(expert_count, capacity, hidden_width), '...]
  transfers between devices with their start and end apart: 4 -> 7, of which waited for: 2 -> 1; matrix products, arithmetic and copies ran while one was open for 9% -> 13% of each run, Pallas kernels for 33% -> 60%
where the time goes in v2:
time: 398 us; the launch traced here: 394 us
  Pallas kernels  265 us (67%)
  matrix products  59.8 us (15%)
  waiting for transfers between devices  28.1 us (7%)
  starting transfers between devices  14.3 us (4%)
  between operations  14.3 us (4%)
  other arithmetic  6.92 us (2%)
  local copies, waits for them, and re-layouts  6.15 us (2%)
    pallas_call x1, Pallas kernels, first_exchange(): pl.pallas_call(functools.partial(first_kernel, groups, experts), out_shap...  139 us
    pallas_call x3, Pallas kernels, expert_exchange(): pl.pallas_call(functools.partial(second_kernel, experts), out_shape=jax.S...  125 us
    ppermute x1, waiting for transfers between devices, local(): rows_in = lax.ppermute(rows_late, 'dp', inward)  27.4 us
    dot_general x8, matrix products, against(): lax.dot_general(taken, weight_part, (((1,), (1,)), ((), ())), preferred_e...  18.4 us
    dot_general x1, matrix products, local(): lax.dot_general(own_piece, block_grad, (((1,), (1,)), ((), ())), preferre...  11.5 us
    dot_general x1, matrix products, local(): lax.dot_general(columns.reshape(-1, half_width), hidden_slots, (((0,), (0...  9.39 us
  transfers between devices with their start and end apart: 7, of which 1 were waited for; matrix products, arithmetic and copies ran while one was open for 13% of the time, Pallas kernels for 60%

profile of v2, /device:TPU:1, one launch (start us, length us, event | category | flops | bytes accessed | tf_op | source)
XLA Modules:
  0.0 394.3 jit_solution(10605428923885525635)
XLA Ops:
  7.9 4.2 %collective-permute-start = (bf16[1024,1024]{1,0:T(8,128)(2,1)}, bf16[1024,1024]{1,0:T(8,128)(2,1)S(1)}, u32[]{:S(2)}, u32[]{:S(2)}) collective-permute-start(bf16[1024,1024]{1,0:T(8,128)(2,1)} %bitcast.80), channel_id=1, source_target_pairs={{0,8},{24,16},{1,9},{25,17},{2,10},{26,18},{3,11},{27,19},{4,12},{... | collective-permute-start | bytes 6291464 | tf_op jit(solution)/shard_map/ppermute | solution.py:167
  12.1 1.0 fusion.5
  13.8 4.9 %convolution_convert_fusion.1 = bf16[512,4096]{1,0:T(8,128)(2,1)} fusion(bf16[256,4096]{1,0:T(8,128)(2,1)} %rows.1, s32[256]{0:T(256)S(1)} %multiply_add_fusion.1), kind=kOutput, calls=%fused_computation.4 | convolution fusion | flops 1075970048 | bytes 6292480 | tf_op jit(solution)/shard_map/dot_general | solution.py:152
  18.6 139.4 %first_exchange.1 = (bf16[4,256,1024]{2,1,0:T(8,128)(2,1)}, s32[4,2,128]{2,1,0:T(2,128)}, bf16[8,64,4096]{2,1,0:T(8,128)(2,1)}) custom-call(bf16[256,4096]{1,0:T(8,128)(2,1)} %rows.1, s32[2,128]{1,0:T(2,128)} %bitcast.73, bf16[8,64,4096]{2,1,0:T(8,128)(2,1)} %bitcast.55), custom_call_target="tpu_custom_call" | custom-call | tf_op jit(solution)/shard_map/first_exchange/pallas_call | solution.py:87
  159.6 5.6 %convolution_convert_fusion.2 = bf16[4,512,1024]{2,1,0:T(8,128)(2,1)} fusion(bf16[4,256,1024]{2,1,0:T(8,128)(2,1)} %get-tuple-element.20, s32[4,256]{1,0:T(4,128)S(1)} %convert_add_fusion), kind=kOutput, calls=%fused_computation.9 | convolution fusion | flops 1076363264 | bytes 6295552 | tf_op jit(solution)/shard_map/dot_general | solution.py:179
  165.3 50.2 %shard_map.85 = bf16[4,8,64,1024]{3,2,1,0:T(8,128)(2,1)} custom-call(bf16[4,8,64,1024]{3,2,1,0:T(8,128)(2,1)} %bitcast.56), custom_call_target="tpu_custom_call" | custom-call | bytes 4194304 | tf_op jit(solution)/shard_map/pallas_call | solution.py:124
  215.5 2.6 collective-permute-start.1
  218.1 2.0 collective-permute-start.2
  220.1 2.0 collective-permute-start.3
  222.1 9.4 %convolution_convert_fusion.3 = bf16[1024,1024]{1,0:T(8,128)(2,1)} fusion(bf16[2048,1024]{1,0:T(8,128)(2,1)} %bitcast.62, bf16[2048,1024]{1,0:T(8,128)(2,1)} %all-gather.2.cloned.1.call-done), kind=kOutput, calls=%fused_computation.18 | convolution fusion | flops 4296015872 | bytes 10485760 | tf_op jit(solution)/shard_map/dot_general | solution.py:192
  231.5 2.3 collective-permute-start.4
  234.8 27.4 %collective-permute-done.1 = bf16[256,4096]{1,0:T(8,128)(2,1)} collective-permute-done((bf16[256,4096]{1,0:T(8,128)(2,1)S(1)}, bf16[256,4096]{1,0:T(8,128)(2,1)}, u32[]{:S(2)}, u32[]{:S(2)}) %collective-permute-start.1) | collective-permute-done | bytes 2097184 | tf_op jit(solution)/shard_map/ppermute | solution.py:173
  262.3 4.9 %convolution_convert_fusion = bf16[512,4096]{1,0:T(8,128)(2,1)} fusion(bf16[256,4096]{1,0:T(8,128)(2,1)} %collective-permute-done.1, s32[256]{0:T(256)S(1)} %multiply_add_fusion), kind=kOutput, calls=%fused_computation.3 | convolution fusion | flops 1075970048 | bytes 6292480 | tf_op jit(solution)/shard_map/dot_general | solution.py:242
  267.1 48.7 %shard_map.86 = bf16[1,8,64,4096]{3,2,1,0:T(8,128)(2,1)} custom-call(bf16[1,8,64,4096]{3,2,1,0:T(8,128)(2,1)} %bitcast.57), custom_call_target="tpu_custom_call" | custom-call | bytes 134217728 | tf_op jit(solution)/shard_map/pallas_call | solution.py:124
  315.9 2.7 fusion.25
  319.1 1.3 fusion.23
  320.4 0.9 copy-done.1
  321.2 1.3 fusion.15
  322.5 2.9 fusion.21
  325.4 2.9 fusion.11
  328.3 3.2 add_convert_fusion.1
  331.5 1.3 fusion.13
  332.8 2.9 add_convert_fusion
  335.7 1.5 pad_maximum_fusion.3.slots
  337.2 26.2 %shard_map.87 = bf16[2,8,64,1024]{3,2,1,0:T(8,128)(2,1)} custom-call(bf16[2,8,64,1024]{3,2,1,0:T(8,128)(2,1)} %pad_maximum_fusion.3.slots), custom_call_target="tpu_custom_call" | custom-call | bytes 67108864 | tf_op jit(solution)/shard_map/pallas_call | solution.py:124
  363.4 1.8 fusion.68
  365.2 1.2 gather_fusion.1
  366.4 1.3 collective-permute-start.5
  367.7 1.2 gather_fusion
  368.8 2.5 broadcast_select_fusion.1
  371.4 11.5 %bitcast_add_fusion = f32[1,1024,2048]{2,1,0:T(8,128)} fusion(f32[1,1024,2048]{2,1,0:T(8,128)} %param.11, bf16[1024,1024]{1,0:T(8,128)(2,1)} %convolution_convert_fusion.3, bf16[1024,1024]{1,0:T(8,128)(2,1)S(1)} %get-tuple-element.30, bf16[1024,1024]{1,0:T(8,128)(2,1)S(1)} %get-tuple-element.29), kind=kOutput, calls=%fused_computation.2 | convolution fusion | flops 4309647360 | bytes 23068672 | tf_op jit(solution)/shard_map/dot_general | solution.py:207
  382.9 3.7 bitcast_add_fusion.1
  (37 shorter events, 5.4 us)
Async XLA Ops:
  7.2 214.9 %all-gather.2.cloned.1.call-start = ((), (), s32[]{:S(2)}) async-start(), calls=%async_computation | async-start | bytes 5242880 | tf_op jit(solution)/shard_map/all_gather | solution.py:150
  7.9 151.7 %collective-permute-start = (bf16[1024,1024]{1,0:T(8,128)(2,1)}, bf16[1024,1024]{1,0:T(8,128)(2,1)S(1)}, u32[]{:S(2)}, u32[]{:S(2)}) collective-permute-start(bf16[1024,1024]{1,0:T(8,128)(2,1)} %bitcast.80), channel_id=1, source_target_pairs={{0,8},{24,16},{1,9},{25,17},{2,10},{26,18},{3,11},{27,19},{4,12},{... | collective-permute-start | bytes 6291464 | tf_op jit(solution)/shard_map/ppermute | solution.py:167
  159.6 5.6 %copy-start.6 = (bf16[1024,1024]{1,0:T(8,128)(2,1)}, bf16[1024,1024]{1,0:T(8,128)(2,1)S(1)}, u32[]{:S(2)}) copy-start(bf16[1024,1024]{1,0:T(8,128)(2,1)S(1)} %collective-permute-done) | copy-start | bytes 6291460
  165.3 50.3 %copy-start = (bf16[256,4096]{1,0:T(8,128)(2,1)S(1)}, bf16[256,4096]{1,0:T(8,128)(2,1)}, u32[]{:S(2)}) copy-start(bf16[256,4096]{1,0:T(8,128)(2,1)} %rows.1) | copy-start | bytes 6291460
  215.5 46.7 %collective-permute-start.1 = (bf16[256,4096]{1,0:T(8,128)(2,1)S(1)}, bf16[256,4096]{1,0:T(8,128)(2,1)}, u32[]{:S(2)}, u32[]{:S(2)}) collective-permute-start(bf16[256,4096]{1,0:T(8,128)(2,1)S(1)} %copy-done), channel_id=1, source_target_pairs={{0,8},{24,16},{1,9},{25,17},{2,10},{26,18},{3,11},{27,19},{4,12},{... | collective-permute-start | bytes 6291464 | tf_op jit(solution)/shard_map/ppermute | solution.py:173
  218.1 102.2 %collective-permute-start.2 = (bf16[1024,1024]{1,0:T(8,128)(2,1)}, bf16[1024,1024]{1,0:T(8,128)(2,1)}, u32[]{:S(2)}, u32[]{:S(2)}) collective-permute-start(bf16[1024,1024]{1,0:T(8,128)(2,1)} %bitcast.81), channel_id=1, source_target_pairs={{8,16},{16,8},{9,17},{17,9},{10,18},{18,10},{11,19},{19,11},{12,20... | collective-permute-start | bytes 6291464 | tf_op jit(solution)/shard_map/ppermute | solution.py:171
  220.1 100.3 %collective-permute-start.3 = (bf16[1024,1024]{1,0:T(8,128)(2,1)}, bf16[1024,1024]{1,0:T(8,128)(2,1)}, u32[]{:S(2)}, u32[]{:S(2)}) collective-permute-start(bf16[1024,1024]{1,0:T(8,128)(2,1)} %copy-done.6), channel_id=1, source_target_pairs={{8,16},{16,8},{9,17},{17,9},{10,18},{18,10},{11,19},{19,11},{12,20... | collective-permute-start | bytes 6291464 | tf_op jit(solution)/shard_map/ppermute | solution.py:172
  222.1 12.7 %copy-start.3 = (s32[256,1]{0,1:T(1,128)S(1)}, s32[256,1]{0,1:T(1,128)}, u32[]{:S(2)}) copy-start(s32[256,1]{0,1:T(1,128)} %param.7) | copy-start | bytes 3076
  231.5 88.9 %collective-permute-start.4 = (bf16[1024,1024]{1,0:T(8,128)(2,1)}, bf16[1024,1024]{1,0:T(8,128)(2,1)}, u32[]{:S(2)}, u32[]{:S(2)}) collective-permute-start(bf16[1024,1024]{1,0:T(8,128)(2,1)} %convolution_convert_fusion.3), channel_id=1, source_target_pairs={{0,8},{8,0},{16,24},{24,16},{1,9},{9,1},{17,25},{25,17},{2,10},{10... | collective-permute-start | bytes 6291464 | tf_op jit(solution)/shard_map/ppermute | solution.py:17
  267.1 48.7 %copy-start.4 = (bf16[1,1024,1024]{2,1,0:T(8,128)(2,1)S(1)}, bf16[1,1024,1024]{2,1,0:T(8,128)(2,1)}, u32[]{:S(2)}) copy-start(bf16[1,1024,1024]{2,1,0:T(8,128)(2,1)} %param.9) | copy-start | bytes 6291460
  315.9 2.7 copy-start.2
  315.9 3.2 copy-start.7
  319.0 2.2 copy-start.1
  366.4 20.2 %collective-permute-start.5 = (bf16[256,1024]{1,0:T(8,128)(2,1)S(1)}, bf16[256,1024]{1,0:T(8,128)(2,1)S(1)}, u32[]{:S(2)}, u32[]{:S(2)}) collective-permute-start(bf16[256,1024]{1,0:T(8,128)(2,1)S(1)} %gather_fusion.1), channel_id=1, source_target_pairs={{8,0},{16,24},{9,1},{17,25},{10,2},{18,26},{11,3},{19,27},{12,4},{... | collective-permute-start | bytes 1572872 | tf_op jit(solution)/shard_map/ppermute | solution.py:268
  371.3 11.5 %copy-start.5 = (f32[1,512,1024]{2,1,0:T(8,128)S(1)}, f32[1,512,1024]{2,1,0:T(8,128)}, u32[]{:S(2)}) copy-start(f32[1,512,1024]{2,1,0:T(8,128)} %param.10) | copy-start | bytes 6291460
Sparse Core Ops, SparseCore 0:
  9.5 146.0 all-gather.1
